TPU v7x, 32 devices: a whole 2x2x4 slice. The times are simulated.
32 devices in a mesh: rows: 16 (over z, x, core), cols: 2 (over y).
Axes of the slice: x: 2, y: 2, z: 4, core: 2. Of those that a mesh axis runs over, the one named last changes fastest.
Arguments:
- kernel: float32 [16384, 1536], P('rows', 'cols'), may hold values from -0.15625 to 0.15625
- row_orbitals: float32 [16384, 512], P('rows', 'cols'), may hold values from -1.5 to 1.5
- col_orbitals: float32 [1536, 512], P('cols', 'rows'), may hold values from -1.5 to 1.5
- col_vectors: float32 [1536, 512], P('cols', 'rows'), may hold values from -6 to 6
Outputs:
- exchange: float32 [512, 16384], P('cols', 'rows')
All inputs are finite; a program needn't handle non-finite values.
Results may differ from a plain program's by a relative error of at most 0.0003.
Values sent between devices are 32-bit elements; how exact they have to be, the bound alone decides.
A program may use at most 64 MiB of HBM per device.

v0:
```python
import jax
import jax.numpy as jnp
from jax import lax
from jax.sharding import PartitionSpec as P


def body(kernel, row_orbitals, col_orbitals, col_vectors):
    full_rows = lax.all_gather(row_orbitals, "cols", axis=1, tiled=True)
    full_cols = lax.all_gather(col_orbitals, "rows", axis=1, tiled=True)
    full_vecs = lax.all_gather(col_vectors, "rows", axis=1, tiled=True)
    gram = jnp.dot(
        full_rows, full_cols.T, precision=lax.Precision.HIGHEST, preferred_element_type=jnp.float32
    )
    weighted = kernel * gram
    return lax.psum_scatter(
        -jnp.dot(
            full_vecs.T,
            weighted.T,
            precision=lax.Precision.HIGHEST,
            preferred_element_type=jnp.float32,
        ),
        "cols",
        scatter_dimension=0,
        tiled=True,
    )


def solution(mesh):
    in_specs = (P("rows", "cols"), P("rows", "cols"), P("cols", "rows"), P("cols", "rows"))
    out_specs = P("cols", "rows")
    return jax.shard_map(body, mesh=mesh, in_specs=in_specs, out_specs=out_specs, check_vma=False)
```

profile of v0, /device:TPU:0, one launch (start us, length us, event | category | flops | bytes accessed | tf_op | source)
XLA Modules:
  0.0 175.4 jit_solution(11052527146017626073)
XLA Ops:
  6.5 0.0 all-gather.4.cloned.1.call-start
  6.5 0.7 all-gather.4.cloned.1.call-update
  7.3 0.0 all-gather.6.cloned.1.call-start
  7.3 0.7 all-gather.6.cloned.1.call-update
  8.0 0.0 all-gather.8.cloned.1.call-start
  8.1 0.7 all-gather.8.cloned.1.call-update
  8.7 0.0 reduce-scatter.2.cloned.1.call-start
  8.8 35.9 %all-gather.4.cloned.1.call-done = f32[1024,512]{1,0:T(8,128)} async-done(((f32[1024,256]{1,0:T(8,128)}), f32[1024,512]{1,0:T(8,128)}) %all-gather.4.cloned.1.call-update) | async-done | bytes 2097168 | tf_op jit(solution)/shard_map/all_gather | solution.py:8
  44.7 41.9 %all-gather.6.cloned.1.call-done = f32[768,512]{0,1:T(8,128)} async-done(((f32[768,32]{0,1:T(8,128)}), f32[768,512]{0,1:T(8,128)}) %all-gather.6.cloned.1.call-update) | async-done | bytes 1572880 | tf_op jit(solution)/shard_map/all_gather | solution.py:9
  86.6 7.2 %fusion.4 = f32[1024,768]{1,0:T(8,128)S(1)} fusion(f32[1024,512]{1,0:T(8,128)} %all-gather.4.cloned.1.call-done, f32[768,512]{0,1:T(8,128)} %all-gather.6.cloned.1.call-done), kind=kOutput, calls=%fused_computation.3 | convolution fusion | flops 4831838208 | bytes 6815744 | tf_op jit(solution)/shard_map/dot_general | solution.py:11
  93.9 33.4 %all-gather.8.cloned.1.call-done = f32[768,512]{0,1:T(8,128)} async-done(((f32[768,32]{0,1:T(8,128)}), f32[768,512]{0,1:T(8,128)}) %all-gather.8.cloned.1.call-update) | async-done | bytes 1572880 | tf_op jit(solution)/shard_map/all_gather | solution.py:10
  127.3 8.3 %negate_bitcast_fusion = f32[512,1024]{0,1:T(8,128)} fusion(f32[768,512]{0,1:T(8,128)} %all-gather.8.cloned.1.call-done, f32[1024,768]{1,0:T(8,128)} %param.4, f32[1024,768]{1,0:T(8,128)S(1)} %fusion.4), kind=kOutput, calls=%fused_computation.2 | convolution fusion | flops 4833148928 | bytes 9961472 | tf_op jit(solution)/shard_map/dot_general | solution.py:16
  135.6 0.0 reduce-scatter.2.cloned.1.call-update
  135.6 30.8 %reduce-scatter.2.cloned.1.call-done = f32[256,1024]{0,1:T(8,128)} async-done(((f32[512,1024]{0,1:T(8,128)}), f32[256,1024]{0,1:T(8,128)}) %reduce-scatter.2.cloned.1.call-update) | async-done | bytes 1048592 | tf_op jit(solution)/shard_map/reduce_scatter | solution.py:15
  166.4 2.5 %copy.5 = f32[256,1024]{1,0:T(8,128)} copy(f32[256,1024]{0,1:T(8,128)} %reduce-scatter.2.cloned.1.call-done) | data formatting | bytes 2097152 | tf_op jit(solution)/shard_map/reduce_scatter | solution.py:15
Async XLA Ops:
  6.5 38.2 %all-gather.4.cloned.1.call-start = ((), (), s32[]{:S(2)}) async-start(), calls=%async_computation.1 | async-start | bytes 3145728 | tf_op jit(solution)/shard_map/all_gather | solution.py:8
  7.3 79.4 %all-gather.6.cloned.1.call-start = ((), (), s32[]{:S(2)}) async-start(), calls=%async_computation.2 | async-start | bytes 1671168 | tf_op jit(solution)/shard_map/all_gather | solution.py:9
  8.0 119.3 %all-gather.8.cloned.1.call-start = ((), (), s32[]{:S(2)}) async-start(), calls=%async_computation.3 | async-start | bytes 1671168 | tf_op jit(solution)/shard_map/all_gather | solution.py:10
  8.7 157.6 %reduce-scatter.2.cloned.1.call-start = ((), (), s32[]{:S(2)}) async-start(), calls=%async_computation.4 | async-start | bytes 3145728 | tf_op jit(solution)/shard_map/reduce_scatter | solution.py:15
Sparse Core Ops, SparseCore 0:
  8.9 35.8 all-gather.3
  47.0 39.5 all-gather.5
  88.9 38.2 all-gather.7
  135.7 30.6 reduce-scatter.1
where the time goes:
time: 176 us; the launch traced here: 175 us
  waiting for transfers between devices  144 us (82%)
  matrix products  15.6 us (9%)
  between operations  13.1 us (7%)
  local copies, waits for them, and re-layouts  2.53 us (1%)
    all_gather x1, waiting for transfers between devices, body(): full_cols = lax.all_gather(col_orbitals, 'rows', axis=1, tiled=True)  41.9 us
    all_gather x1, waiting for transfers between devices, body(): full_rows = lax.all_gather(row_orbitals, 'cols', axis=1, tiled=True)  35.9 us
    all_gather x1, waiting for transfers between devices, body(): full_vecs = lax.all_gather(col_vectors, 'rows', axis=1, tiled=True)  33.4 us
    reduce_scatter x1, waiting for transfers between devices, body(): lax.psum_scatter(-jnp.dot(full_vecs.T, weighted.T, precision=lax.Precisio...  30.8 us
    dot_general x1, matrix products, body(): jnp.dot(full_vecs.T, weighted.T, precision=lax.Precision.HIGHEST, preferr...  8.31 us
    dot_general x1, matrix products, body(): jnp.dot(full_rows, full_cols.T, precision=lax.Precision.HIGHEST, preferre...  7.25 us
  transfers between devices with their start and end apart: 4, of which 4 were waited for; matrix products, arithmetic and copies ran while one was open for 4% of the time, Pallas kernels for 0%

commit v1 on v0

v1 whole, which is shorter than its diff:
```python
import functools

import jax
import jax.numpy as jnp
from jax import lax
from jax.experimental import pallas as pl
from jax.experimental.pallas import tpu as pltpu
from jax.sharding import PartitionSpec as P

MESH = pl.DeviceIdType.MESH
LEFT, RIGHT, PAIR, CORE = range(4)


def split(x):
    hi = x.astype(jnp.bfloat16)
    return hi, (x - hi.astype(jnp.float32)).astype(jnp.bfloat16)


def dot3(a_hi, a_lo, b_hi, b_lo, dims):
    dot = functools.partial(lax.dot_general, dimension_numbers=(dims, ((), ())), preferred_element_type=jnp.float32)
    return dot(a_lo, b_hi) + dot(a_hi, b_lo) + dot(a_hi, b_hi)


def exchange_kernel(
    nr, nc, chunks,
    k_hbm, row_hbm, orb_hbm, vec_hbm, out_ref,
    k, rows, orb, vec, orb_hi, orb_lo, vec_hi, vec_lo, theirs, got, mine,
    local_sem, row_send, row_recv, col_send, col_recv, out_send, out_recv,
):
    r, c = lax.axis_index("rows"), lax.axis_index("cols")
    core, chip = lax.rem(r, 2), r // 2
    pair, line, lines = lax.rem(chip, 2), chip // 2, nr // 4
    per = orb_hbm.shape[0]
    chunk = row_hbm.shape[0] // chunks
    mb = row_hbm.shape[1]
    nb = theirs.shape[2]

    def at(l, p, q):
        return (l * 2 + p) * 2 + q

    goal = {
        LEFT: at(line - 1, pair, core),
        RIGHT: at(line + 1, pair, core),
        PAIR: at(line, 1 - pair, core),
        CORE: at(line, pair, 1 - core),
    }
    has_left, has_right = line > 0, line < lines - 1

    barrier = pltpu.get_barrier_semaphore()

    def greet(row, col):
        pl.semaphore_signal(barrier, inc=1, device_id=(row, col), device_id_type=MESH)

    for j in range(1, nc):
        greet(r, lax.rem(c + j, nc))
    greet(goal[PAIR], c)
    greet(goal[CORE], c)
    pl.when(has_left)(lambda: greet(goal[LEFT], c))
    pl.when(has_right)(lambda: greet(goal[RIGHT], c))

    k_copy = pltpu.make_async_copy(k_hbm, k, local_sem.at[0])
    row_copy = pltpu.make_async_copy(row_hbm, rows.at[0], local_sem.at[1])
    own = pl.ds(pl.multiple_of(r * per, per), per)
    orb_copy = pltpu.make_async_copy(orb_hbm, orb.at[own], local_sem.at[2])
    vec_copy = pltpu.make_async_copy(vec_hbm, vec.at[own], local_sem.at[3])
    for copy in (k_copy, row_copy, orb_copy, vec_copy):
        copy.start()

    pl.semaphore_wait(barrier, nc - 1 + 2 + has_left.astype(jnp.int32) + has_right.astype(jnp.int32))

    def row_chunk(j, i):
        at_rows = pl.ds(i * chunk, chunk) if isinstance(i, int) else pl.ds(pl.multiple_of(i * chunk, chunk), chunk)
        return pltpu.make_async_remote_copy(
            src_ref=row_hbm.at[at_rows],
            dst_ref=rows.at[j, at_rows],
            send_sem=row_send.at[j - 1, i],
            recv_sem=row_recv.at[j - 1, i],
            device_id=(r, lax.rem(c + j, nc)),
            device_id_type=MESH,
        )

    for i in range(chunks):
        for j in range(1, nc):
            row_chunk(j, i).start()

    def shard(t, s, way, first=False):
        full = (orb, vec)[t]
        there = full.at[pl.ds(pl.multiple_of(s * per, per), per)]
        return pltpu.make_async_remote_copy(
            src_ref=(orb_hbm, vec_hbm)[t] if first else there,
            dst_ref=there,
            send_sem=col_send.at[t, way, s],
            recv_sem=col_recv.at[t, s],
            device_id=(goal[way], c),
            device_id_type=MESH,
        )

    def line_sources(d):
        if d == 0:
            return [(line, None, ((LEFT, has_left), (RIGHT, has_right), (PAIR, None), (CORE, None)))]
        return [
            (line - d, line - d >= 0, ((RIGHT, has_right), (PAIR, None), (CORE, None))),
            (line + d, line + d < lines, ((LEFT, has_left), (PAIR, None), (CORE, None))),
        ]

    def when(cond, do):
        if cond is None:
            do()
        else:
            pl.when(cond)(do)

    def pass_on(op, t, d):
        for l, there, ways in line_sources(d):
            def go(l=l, ways=ways):
                s = at(l, pair, core)
                if op == "start" and d > 0:
                    shard(t, s, PAIR).wait_recv()
                for way, cond in ways:
                    copy = shard(t, s, way, d == 0)
                    when(cond, copy.start if op == "start" else copy.wait_send)
            when(there, go)

    def pass_over(op, t, d):
        for l, there, _ in line_sources(d):
            def go(l=l):
                s = at(l, 1 - pair, core)
                copy = shard(t, s, CORE)
                if op == "start":
                    copy.wait_recv()
                    copy.start()
                else:
                    copy.wait_send()
            when(there, go)

    for d in range(lines):
        for t in range(2):
            pass_on("start", t, d)
        if d > 0:
            for t in range(2):
                pass_over("start", t, d - 1)
    for t in range(2):
        pass_over("start", t, lines - 1)

    k_copy.wait()
    row_copy.wait()
    orb_copy.wait()
    vec_copy.wait()
    for t in range(2):
        for l in range(lines):
            for p in range(2):
                shard(t, at(l, p, 1 - core), CORE).wait_recv()

        @pl.loop(0, nr)
        def _(s, t=t):
            here = pl.ds(pl.multiple_of(s * per, per), per)
            if t == 0:
                orb_hi[here], orb_lo[here] = split(orb[here])
            else:
                vec_hi[here], vec_lo[here] = split(-vec[here])

    def out_chunk(j, i):
        return pltpu.make_async_remote_copy(
            src_ref=theirs.at[j - 1, i],
            dst_ref=got.at[j - 1, i],
            send_sem=out_send.at[j - 1, i],
            recv_sem=out_recv.at[j - 1, i],
            device_id=(r, lax.rem(c + j, nc)),
            device_id_type=MESH,
        )

    @pl.loop(0, chunks)
    def _(i):
        here = pl.ds(pl.multiple_of(i * chunk, chunk), chunk)
        gram = None
        for j in range(nc):
            if j > 0:
                row_chunk(j, i).wait_recv()
            block = pl.ds(pl.multiple_of(lax.rem(c - j + nc, nc) * mb, mb), mb)
            term = dot3(*split(rows[j, here, :]), orb_hi[block], orb_lo[block], ((1,), (0,)))
            gram = term if gram is None else gram + term
        w_hi, w_lo = split(k[here] * gram)
        for j in list(range(1, nc)) + [0]:
            block = pl.ds(pl.multiple_of(lax.rem(c + j, nc) * nb, nb), nb)
            part = dot3(vec_hi[block], vec_lo[block], w_hi, w_lo, ((1,), (1,)))
            if j == 0:
                mine[i] = part
            else:
                theirs[j - 1, i] = part
                out_chunk(j, i).start()

    for t in range(2):
        for d in range(lines):
            pass_on("wait", t, d)
            pass_over("wait", t, d)
    for i in range(chunks):
        for j in range(1, nc):
            row_chunk(j, i).wait_send()

    for i in range(chunks):
        total = mine[i]
        for j in range(1, nc):
            out_chunk(j, i).wait_recv()
            total = total + got[j - 1, i]
        out_ref[:, i * chunk:(i + 1) * chunk] = total
    for i in range(chunks):
        for j in range(1, nc):
            out_chunk(j, i).wait_send()


def solution(mesh):
    nr, nc = mesh.shape["rows"], mesh.shape["cols"]

    def body(kernel, row_orbitals, col_orbitals, col_vectors):
        n_rows, n_cols = kernel.shape
        mb, per = row_orbitals.shape[1], col_orbitals.shape[1]
        norb = mb * nc
        nb = norb // nc
        chunks = n_rows // 128
        chunk = n_rows // chunks
        f32, bf16, dma = jnp.float32, jnp.bfloat16, pltpu.SemaphoreType.DMA
        return pl.pallas_call(
            functools.partial(exchange_kernel, nr, nc, chunks),
            out_shape=jax.ShapeDtypeStruct((nb, n_rows), f32),
            in_specs=[pl.BlockSpec(memory_space=pl.ANY)] * 4,
            out_specs=pl.BlockSpec(memory_space=pltpu.VMEM),
            scratch_shapes=[
                pltpu.VMEM((n_rows, n_cols), f32),
                pltpu.VMEM((nc, n_rows, mb), f32),
                pltpu.VMEM((norb, n_cols), f32),
                pltpu.VMEM((norb, n_cols), f32),
                pltpu.VMEM((norb, n_cols), bf16),
                pltpu.VMEM((norb, n_cols), bf16),
                pltpu.VMEM((norb, n_cols), bf16),
                pltpu.VMEM((norb, n_cols), bf16),
                pltpu.VMEM((nc - 1, chunks, nb, chunk), f32),
                pltpu.VMEM((nc - 1, chunks, nb, chunk), f32),
                pltpu.VMEM((chunks, nb, chunk), f32),
                dma((4,)),
                dma((nc - 1, chunks)),
                dma((nc - 1, chunks)),
                dma((2, 4, nr)),
                dma((2, nr)),
                dma((nc - 1, chunks)),
                dma((nc - 1, chunks)),
            ],
            compiler_params=pltpu.CompilerParams(
                collective_id=0, has_side_effects=True, vmem_limit_bytes=60 * 1024 * 1024
            ),
        )(kernel, row_orbitals, col_orbitals.T, col_vectors.T)

    in_specs = (P("rows", "cols"), P("rows", "cols"), P("cols", "rows"), P("cols", "rows"))
    out_specs = P("cols", "rows")
    return jax.shard_map(body, mesh=mesh, in_specs=in_specs, out_specs=out_specs, check_vma=False)
```

time: 176 us -> 55.2 us (0.31)
  waiting for transfers between devices: 144 us -> 0 us
  Pallas kernels: 0 us -> 52.7 us
  matrix products: 15.6 us -> 0 us
  between operations: 13.1 us -> 0.01 us
    all_gather x3 -> x0, waiting for transfers between devices: 111 us -> none  [the longest x1 41.9 us: body(): full_cols = lax.all_gather(col_orbitals, 'rows', axis=1, tiled=True)]
    pallas_call x0 -> x1, Pallas kernels: none -> 52.7 us  [body(): pl.pallas_call(functools.partial(exchange_kernel, nr, nc, chunks), out_sh...]
    reduce_scatter x1 -> x0, waiting for transfers between devices: 30.8 us -> none  [body(): lax.psum_scatter(-jnp.dot(full_vecs.T, weighted.T, precision=lax.Precisio...]
    dot_general x2 -> x0, matrix products: 15.6 us -> none  [the longest x1 8.31 us: body(): jnp.dot(full_vecs.T, weighted.T, precision=lax.Precision.HIGHEST, preferr...]
    reduce_scatter x1 -> x0, local copies, waits for them, and re-layouts: 2.53 us -> none  [body(): lax.psum_scatter(-jnp.dot(full_vecs.T, weighted.T, precision=lax.Precisio...]
    unnamed x0 -> x1, local copies, waits for them, and re-layouts: none -> 2.31 us
    unnamed x4 -> x0, waiting for transfers between devices: 2.1 us -> none
  transfers between devices with their start and end apart: 4 -> 0, of which waited for: 4 -> 0; matrix products, arithmetic and copies ran while one was open for 4% -> 0% of each run, Pallas kernels for 0% -> 0%
where the time goes in v1:
time: 55.2 us; the launch traced here: 55 us
  Pallas kernels  52.7 us (95%)
  local copies, waits for them, and re-layouts  2.31 us (4%)
    pallas_call x1, Pallas kernels, body(): pl.pallas_call(functools.partial(exchange_kernel, nr, nc, chunks), out_sh...  52.7 us
    unnamed x1, local copies, waits for them, and re-layouts  2.31 us

profile of v1, /device:TPU:0, one launch (start us, length us, event | category | flops | bytes accessed | tf_op | source)
XLA Modules:
  0.0 55.0 jit_solution(7951065828696199613)
XLA Ops:
  0.0 52.7 %shard_map.46 = f32[256,1024]{1,0:T(8,128)} custom-call(f32[1024,768]{1,0:T(8,128)} %k_hbm.1, f32[1024,256]{1,0:T(8,128)} %row_hbm.1, f32[32,768]{1,0:T(8,128)} %bitcast.2, f32[32,768]{1,0:T(8,128)} %bitcast.3), custom_call_target="tpu_custom_call" | custom-call | tf_op jit(solution)/shard_map/pallas_call | solution.py:221
  52.7 2.3 %copy.6 = f32[256,1024]{1,0:T(8,128)} copy(f32[256,1024]{1,0:T(8,128)} %shard_map.46) | data formatting | bytes 2097152

commit v2 on v1

--- a/solution.py
+++ b/solution.py
@@ -220,7 +220,7 @@
         f32, bf16, dma = jnp.float32, jnp.bfloat16, pltpu.SemaphoreType.DMA
         return pl.pallas_call(
             functools.partial(exchange_kernel, nr, nc, chunks),
-            out_shape=jax.ShapeDtypeStruct((nb, n_rows), f32),
+            out_shape=pltpu.VMEM((nb, n_rows), f32),
             in_specs=[pl.BlockSpec(memory_space=pl.ANY)] * 4,
             out_specs=pl.BlockSpec(memory_space=pltpu.VMEM),
             scratch_shapes=[

time: 55.2 us -> 52.8 us (0.957)
  local copies, waits for them, and re-layouts: 2.31 us -> 0.97 us
  Pallas kernels: 52.7 us -> 51.7 us
    unnamed x1, local copies, waits for them, and re-layouts: 2.31 us -> 0.97 us
    pallas_call x1, Pallas kernels: 52.7 us -> 51.7 us  [body(): pl.pallas_call(functools.partial(exchange_kernel, nr, nc, chunks), out_sh...]
where the time goes in v2:
time: 52.8 us; the launch traced here: 52.7 us
  Pallas kernels  51.7 us (98%)
  local copies, waits for them, and re-layouts  0.97 us (2%)
    pallas_call x1, Pallas kernels, body(): pl.pallas_call(functools.partial(exchange_kernel, nr, nc, chunks), out_sh...  51.7 us

profile of v2, /device:TPU:0, one launch (start us, length us, event | category | flops | bytes accessed | tf_op | source)
XLA Modules:
  0.0 52.7 jit_solution(2596229566745341161)
XLA Ops:
  0.0 51.7 %shard_map.46 = f32[256,1024]{1,0:T(8,128)S(1)} custom-call(f32[1024,768]{1,0:T(8,128)} %k_hbm.1, f32[1024,256]{1,0:T(8,128)} %row_hbm.1, f32[32,768]{1,0:T(8,128)} %bitcast.2, f32[32,768]{1,0:T(8,128)} %bitcast.3), custom_call_target="tpu_custom_call" | custom-call | tf_op jit(solution)/shard_map/pallas_call | solution.py:221
  51.7 1.0 %copy.6 = f32[256,1024]{1,0:T(8,128)} copy(f32[256,1024]{1,0:T(8,128)S(1)} %shard_map.46) | data formatting | bytes 2097152

commit v3 on v2

--- a/solution.py
+++ b/solution.py
@@ -25,7 +25,7 @@
     nr, nc, chunks,
     k_hbm, row_hbm, orb_hbm, vec_hbm, out_ref,
     k, rows, orb, vec, orb_hi, orb_lo, vec_hi, vec_lo, theirs, got, mine,
-    local_sem, row_send, row_recv, col_send, col_recv, out_send, out_recv,
+    local_sem, row_send, row_recv, col_send, col_recv, core_recv, out_send, out_recv,
 ):
     r, c = lax.axis_index("rows"), lax.axis_index("cols")
     core, chip = lax.rem(r, 2), r // 2
@@ -73,7 +73,7 @@
         return pltpu.make_async_remote_copy(
             src_ref=row_hbm.at[at_rows],
             dst_ref=rows.at[j, at_rows],
-            send_sem=row_send.at[j - 1, i],
+            send_sem=row_send.at[j - 1],
             recv_sem=row_recv.at[j - 1, i],
             device_id=(r, lax.rem(c + j, nc)),
             device_id_type=MESH,
@@ -83,14 +83,13 @@
         for j in range(1, nc):
             row_chunk(j, i).start()
 
-    def shard(t, s, way, first=False):
-        full = (orb, vec)[t]
-        there = full.at[pl.ds(pl.multiple_of(s * per, per), per)]
+    def shard(t, l, p, way, first=False):
+        there = (orb, vec)[t].at[pl.ds(pl.multiple_of(at(l, p, core) * per, per), per)]
         return pltpu.make_async_remote_copy(
             src_ref=(orb_hbm, vec_hbm)[t] if first else there,
             dst_ref=there,
-            send_sem=col_send.at[t, way, s],
-            recv_sem=col_recv.at[t, s],
+            send_sem=col_send.at[way],
+            recv_sem=core_recv.at[0] if way == CORE else col_recv.at[t, p, l],
             device_id=(goal[way], c),
             device_id_type=MESH,
         )
@@ -109,46 +108,48 @@
         else:
             pl.when(cond)(do)
 
-    def pass_on(op, t, d):
+    def pass_on(t, d):
         for l, there, ways in line_sources(d):
             def go(l=l, ways=ways):
-                s = at(l, pair, core)
-                if op == "start" and d > 0:
-                    shard(t, s, PAIR).wait_recv()
+                if d > 0:
+                    shard(t, l, pair, PAIR).wait_recv()
                 for way, cond in ways:
-                    copy = shard(t, s, way, d == 0)
-                    when(cond, copy.start if op == "start" else copy.wait_send)
+                    when(cond, shard(t, l, pair, way, d == 0).start)
             when(there, go)
 
-    def pass_over(op, t, d):
+    def pass_over(t, d):
         for l, there, _ in line_sources(d):
             def go(l=l):
-                s = at(l, 1 - pair, core)
-                copy = shard(t, s, CORE)
-                if op == "start":
-                    copy.wait_recv()
-                    copy.start()
-                else:
-                    copy.wait_send()
+                shard(t, l, 1 - pair, PAIR).wait_recv()
+                shard(t, l, 1 - pair, CORE).start()
             when(there, go)
 
     for d in range(lines):
         for t in range(2):
-            pass_on("start", t, d)
+            pass_on(t, d)
         if d > 0:
             for t in range(2):
-                pass_over("start", t, d - 1)
+                pass_over(t, d - 1)
     for t in range(2):
-        pass_over("start", t, lines - 1)
+        pass_over(t, lines - 1)
+
+    def bulk(way, count):
+        part = orb.at[pl.ds(0, count * per)]
+        return pltpu.make_async_remote_copy(
+            src_ref=part,
+            dst_ref=part,
+            send_sem=col_send.at[way],
+            recv_sem=core_recv.at[0],
+            device_id=(goal[CORE], c),
+            device_id_type=MESH,
+        )
 
     k_copy.wait()
     row_copy.wait()
     orb_copy.wait()
     vec_copy.wait()
+    bulk(CORE, nr).wait_recv()
     for t in range(2):
-        for l in range(lines):
-            for p in range(2):
-                shard(t, at(l, p, 1 - core), CORE).wait_recv()
 
         @pl.loop(0, nr)
         def _(s, t=t):
@@ -162,7 +163,7 @@
         return pltpu.make_async_remote_copy(
             src_ref=theirs.at[j - 1, i],
             dst_ref=got.at[j - 1, i],
-            send_sem=out_send.at[j - 1, i],
+            send_sem=out_send.at[j - 1],
             recv_sem=out_recv.at[j - 1, i],
             device_id=(r, lax.rem(c + j, nc)),
             device_id_type=MESH,
@@ -188,13 +189,13 @@
                 theirs[j - 1, i] = part
                 out_chunk(j, i).start()
 
-    for t in range(2):
-        for d in range(lines):
-            pass_on("wait", t, d)
-            pass_over("wait", t, d)
-    for i in range(chunks):
-        for j in range(1, nc):
-            row_chunk(j, i).wait_send()
+    bulk(PAIR, 2 * lines).wait_send()
+    bulk(CORE, nr).wait_send()
+    for l in range(lines):
+        if l > 0:
+            pl.when(line == l)(bulk(LEFT, 2 * (lines - l)).wait_send)
+        if l < lines - 1:
+            pl.when(line == l)(bulk(RIGHT, 2 * (l + 1)).wait_send)
 
     for i in range(chunks):
         total = mine[i]
@@ -202,9 +203,14 @@
             out_chunk(j, i).wait_recv()
             total = total + got[j - 1, i]
         out_ref[:, i * chunk:(i + 1) * chunk] = total
-    for i in range(chunks):
-        for j in range(1, nc):
-            out_chunk(j, i).wait_send()
+    for j in range(1, nc):
+        peer = {"device_id": (r, lax.rem(c + j, nc)), "device_id_type": MESH}
+        pltpu.make_async_remote_copy(
+            row_hbm, rows.at[j], row_send.at[j - 1], row_recv.at[j - 1, 0], **peer
+        ).wait_send()
+        pltpu.make_async_remote_copy(
+            theirs.at[j - 1], got.at[j - 1], out_send.at[j - 1], out_recv.at[j - 1, 0], **peer
+        ).wait_send()
 
 
 def solution(mesh):
@@ -236,11 +242,12 @@
                 pltpu.VMEM((nc - 1, chunks, nb, chunk), f32),
                 pltpu.VMEM((chunks, nb, chunk), f32),
                 dma((4,)),
+                dma((nc - 1,)),
                 dma((nc - 1, chunks)),
-                dma((nc - 1, chunks)),
-                dma((2, 4, nr)),
-                dma((2, nr)),
-                dma((nc - 1, chunks)),
+                dma((4,)),
+                dma((2, 2, nr // 4)),
+                dma((1,)),
+                dma((nc - 1,)),
                 dma((nc - 1, chunks)),
             ],
             compiler_params=pltpu.CompilerParams(

time: 52.8 us -> 51.2 us (0.970)
  Pallas kernels: 51.7 us -> 50.1 us
    pallas_call x1, Pallas kernels: 51.7 us -> 50.1 us  [body(): pl.pallas_call(functools.partial(exchange_kernel, nr, nc, chunks), out_sh...]
where the time goes in v3:
time: 51.2 us; the launch traced here: 51 us
  Pallas kernels  50.1 us (98%)
  local copies, waits for them, and re-layouts  0.97 us (2%)
    pallas_call x1, Pallas kernels, body(): pl.pallas_call(functools.partial(exchange_kernel, nr, nc, chunks), out_sh...  50.1 us

profile of v3, /device:TPU:0, one launch (start us, length us, event | category | flops | bytes accessed | tf_op | source)
XLA Modules:
  0.0 51.0 jit_solution(15968842543732709535)
XLA Ops:
  0.0 50.1 %shard_map.46 = f32[256,1024]{1,0:T(8,128)S(1)} custom-call(f32[1024,768]{1,0:T(8,128)} %k_hbm.1, f32[1024,256]{1,0:T(8,128)} %row_hbm.1, f32[32,768]{1,0:T(8,128)} %bitcast.2, f32[32,768]{1,0:T(8,128)} %bitcast.3), custom_call_target="tpu_custom_call" | custom-call | tf_op jit(solution)/shard_map/pallas_call | solution.py:227
  50.1 1.0 %copy.6 = f32[256,1024]{1,0:T(8,128)} copy(f32[256,1024]{1,0:T(8,128)S(1)} %shard_map.46) | data formatting | bytes 2097152

commit v4 on v3

--- a/solution.py
+++ b/solution.py
@@ -108,6 +108,13 @@
         else:
             pl.when(cond)(do)
 
+    def keep(t, s):
+        here = pl.ds(pl.multiple_of(s * per, per), per)
+        if t == 0:
+            orb_hi[here], orb_lo[here] = split(orb[here])
+        else:
+            vec_hi[here], vec_lo[here] = split(-vec[here])
+
     def pass_on(t, d):
         for l, there, ways in line_sources(d):
             def go(l=l, ways=ways):
@@ -115,6 +122,8 @@
                     shard(t, l, pair, PAIR).wait_recv()
                 for way, cond in ways:
                     when(cond, shard(t, l, pair, way, d == 0).start)
+                if d > 0:
+                    keep(t, at(l, pair, core))
             when(there, go)
 
     def pass_over(t, d):
@@ -122,6 +131,7 @@
             def go(l=l):
                 shard(t, l, 1 - pair, PAIR).wait_recv()
                 shard(t, l, 1 - pair, CORE).start()
+                keep(t, at(l, 1 - pair, core))
             when(there, go)
 
     for d in range(lines):
@@ -144,20 +154,16 @@
             device_id_type=MESH,
         )
 
-    k_copy.wait()
-    row_copy.wait()
-    orb_copy.wait()
-    vec_copy.wait()
+    for copy in (orb_copy, vec_copy, k_copy, row_copy):
+        copy.wait()
+    for t in range(2):
+        keep(t, r)
     bulk(CORE, nr).wait_recv()
     for t in range(2):
 
-        @pl.loop(0, nr)
-        def _(s, t=t):
-            here = pl.ds(pl.multiple_of(s * per, per), per)
-            if t == 0:
-                orb_hi[here], orb_lo[here] = split(orb[here])
-            else:
-                vec_hi[here], vec_lo[here] = split(-vec[here])
+        @pl.loop(0, nr // 2)
+        def _(m, t=t):
+            keep(t, m * 2 + 1 - core)
 
     def out_chunk(j, i):
         return pltpu.make_async_remote_copy(
@@ -221,7 +227,7 @@
         mb, per = row_orbitals.shape[1], col_orbitals.shape[1]
         norb = mb * nc
         nb = norb // nc
-        chunks = n_rows // 128
+        chunks = n_rows // 256
         chunk = n_rows // chunks
         f32, bf16, dma = jnp.float32, jnp.bfloat16, pltpu.SemaphoreType.DMA
         return pl.pallas_call(

time: 51.2 us -> 51.1 us (level)
  no operation moved by 1% of the time
where the time goes in v4:
time: 51.1 us; the launch traced here: 50.9 us
  Pallas kernels  49.9 us (98%)
  local copies, waits for them, and re-layouts  0.97 us (2%)
    pallas_call x1, Pallas kernels, body(): pl.pallas_call(functools.partial(exchange_kernel, nr, nc, chunks), out_sh...  49.9 us

profile of v4, /device:TPU:0, one launch (start us, length us, event | category | flops | bytes accessed | tf_op | source)
XLA Modules:
  0.0 50.9 jit_solution(9876069361055306659)
XLA Ops:
  0.0 49.9 %shard_map.46 = f32[256,1024]{1,0:T(8,128)S(1)} custom-call(f32[1024,768]{1,0:T(8,128)} %k_hbm.1, f32[1024,256]{1,0:T(8,128)} %row_hbm.1, f32[32,768]{1,0:T(8,128)} %bitcast.2, f32[32,768]{1,0:T(8,128)} %bitcast.3), custom_call_target="tpu_custom_call" | custom-call | tf_op jit(solution)/shard_map/pallas_call | solution.py:233
  49.9 1.0 %copy.6 = f32[256,1024]{1,0:T(8,128)} copy(f32[256,1024]{1,0:T(8,128)S(1)} %shard_map.46) | data formatting | bytes 2097152
